TPU v7x, 32 devices: a whole 2x2x4 slice. The times are simulated.
32 devices in a mesh: rep: 2 (over y), fsdp: 4 (over z), section: 4 (over x, core).
Axes of the slice: x: 2, y: 2, z: 4, core: 2. Of those that a mesh axis runs over, the one named last changes fastest.
Arguments:
- iterate: bfloat16 [8, 3072, 1024], P(('rep', 'section'), None, 'fsdp'), parts along dimension 0, may hold values from -0.1875 to 0.1875
Outputs:
- update: bfloat16 [8, 3072, 1024], P(('rep', 'section'), None, 'fsdp'), parts along dimension 0
There are 2 independent parts, one for each index of `rep`. A program takes and returns all parts, laid end to end along the dimension named above; each array names one. Nothing has to cross between parts.
All inputs are finite; a program needn't handle non-finite values.
Results may differ from a plain program's by a relative error of at most 0.0055.
Values may be sent and summed in bfloat16 or wider, within the bound.
A program may use at most 128 MiB of HBM per device.

v0:
```python
import math
import jax
import jax.numpy as jnp
import numpy as np
from jax import lax
from jax.sharding import PartitionSpec as P


def tile_table(devices, band_blocks):
    block_table = np.zeros((devices, devices), dtype=np.int32)
    for row_block in range(devices):
        for col_block in range(devices):
            distance = (col_block - row_block) % devices
            if distance <= devices // 2:
                block_table[row_block, col_block] = row_block * band_blocks + distance
            else:
                block_table[row_block, col_block] = (
                    devices * band_blocks + col_block * band_blocks + (devices - distance)
                )
    return block_table


def on_device(iterate):
    devices = lax.axis_size("fsdp")
    experts, rows_all, columns = iterate.shape
    strip_rows = rows_all // devices
    band_blocks = devices // 2 + 1
    out_scale = 0.2 * math.sqrt(max(rows_all, columns * devices))
    expert_rows = iterate[0]
    row_blocks = expert_rows.reshape(devices, strip_rows, columns)

    def one_offset(offset):
        partner = jnp.roll(row_blocks, -offset, axis=0)
        tiles = jnp.einsum("nsc,ntc->nst", row_blocks, partner, preferred_element_type=jnp.float32)
        return tiles.astype(jnp.bfloat16)

    band_term = lax.map(one_offset, jnp.arange(band_blocks, dtype=jnp.int32))
    received = lax.all_to_all(band_term, "fsdp", split_axis=1, concat_axis=1, tiled=True)
    own_band = jnp.sum(received.astype(jnp.float32), axis=1).astype(jnp.bfloat16)
    upper_tiles = lax.all_gather(own_band, "fsdp", axis=0, tiled=True)
    tile_pool = jnp.concatenate([upper_tiles, jnp.swapaxes(upper_tiles, 1, 2)], axis=0)
    block_table = jnp.asarray(tile_table(devices, band_blocks))
    dense_blocks = jnp.take(tile_pool, block_table, axis=0)

    def apply_gram(operand):
        shaped = operand.reshape(devices, strip_rows, columns)
        product = jnp.einsum(
            "nmij,mjc->nic", dense_blocks, shaped, preferred_element_type=jnp.float32
        )
        return product.reshape(rows_all, columns)

    first_product = apply_gram(expert_rows)
    second_product = apply_gram(first_product.astype(jnp.bfloat16))
    combined = out_scale * (
        3.4445 * expert_rows.astype(jnp.float32) - 4.775 * first_product + 2.0315 * second_product
    )
    results = [combined.astype(jnp.bfloat16)]
    return jnp.stack(results)


def on_device_columns(iterate):
    devices = lax.axis_size("fsdp")
    own = lax.axis_index("fsdp")
    _, rows_all, columns = iterate.shape
    out_scale = 0.2 * math.sqrt(max(rows_all, columns * devices))
    gathered = lax.all_gather(iterate[0], "fsdp", axis=1, tiled=True)
    gram = lax.dot_general(
        gathered, gathered, (((0,), (0,)), ((), ())), preferred_element_type=jnp.float32
    )
    gram_half = gram.astype(jnp.bfloat16)
    own_gram = lax.dynamic_slice_in_dim(gram, own * columns, columns, 1)
    square = jnp.dot(gram_half, own_gram.astype(jnp.bfloat16), preferred_element_type=jnp.float32)
    row_ids = lax.broadcasted_iota(jnp.int32, square.shape, 0)
    column_ids = lax.broadcasted_iota(jnp.int32, square.shape, 1) + own * columns
    identity = (row_ids == column_ids).astype(jnp.float32)
    mixing = out_scale * (3.4445 * identity - 4.775 * own_gram + 2.0315 * square)
    update = jnp.dot(gathered, mixing.astype(jnp.bfloat16), preferred_element_type=jnp.float32)
    return update.astype(jnp.bfloat16)[None]


def for_shapes(iterate):
    _, rows_all, columns = iterate.shape
    if columns * lax.axis_size("fsdp") <= rows_all:
        return on_device_columns(iterate)
    return on_device(iterate)


def solution(mesh):
    return jax.shard_map(
        for_shapes,
        mesh=mesh,
        in_specs=(P(("rep", "section"), None, "fsdp"),),
        out_specs=P(("rep", "section"), None, "fsdp"),
        check_vma=False,
    )
```

profile of v0, /device:TPU:0, one launch (start us, length us, event | category | flops | bytes accessed | tf_op | source)
XLA Modules:
  0.0 155.0 jit_solution(9944123637097311542)
XLA Ops:
  6.5 0.0 all-gather.3.cloned.1.call-start
  6.5 0.7 all-gather.3.cloned.1.call-update
  7.3 119.2 %all-gather.3.cloned.1.call-done = bf16[1,3072,1024]{2,1,0:T(8,128)(2,1)} async-done(((bf16[1,3072,256]{2,1,0:T(8,128)(2,1)}), bf16[1,3072,1024]{2,1,0:T(8,128)(2,1)}) %all-gather.3.cloned.1.call-update) | async-done | bytes 6291472 | tf_op jit(solution)/shard_map/all_gather | solution.py:66
  126.5 12.0 %fusion.2 = f32[1024,1024]{1,0:T(8,128)} fusion(bf16[1,3072,1024]{2,1,0:T(8,128)(2,1)} %all-gather.3.cloned.1.call-done), kind=kOutput, calls=%fused_computation.2 | convolution fusion | flops 6442450944 | bytes 10485760 | tf_op jit(solution)/shard_map/dot_general | solution.py:67
  138.5 8.1 %fusion.7 = bf16[1,3072,256]{1,2,0:T(8,128)(2,1)S(1)} fusion(bf16[1,3072,1024]{2,1,0:T(8,128)(2,1)} %all-gather.3.cloned.1.call-done, f32[1024,1024]{1,0:T(8,128)} %fusion.2, s32[]{:T(128)S(6)} %select_n.3, s32[256]{0:T(256)S(1)} %iota_add_fusion), kind=kOutput, calls=%fused_computation.5 | convolution fusion | flops 2151677952 | bytes 14157824 | tf_op jit(solution)/shard_map/dot_general | solution.py:77
  146.6 1.6 %copy.2 = bf16[1,3072,256]{2,1,0:T(8,128)(2,1)} copy(bf16[1,3072,256]{1,2,0:T(8,128)(2,1)S(1)} %fusion.7) | data formatting | bytes 3145728 | tf_op jit(solution)/shard_map/broadcast_in_dim | solution.py:78
  (1 shorter events, 0.0 us)
Async XLA Ops:
  6.5 120.0 %all-gather.3.cloned.1.call-start = ((), (), s32[]{:S(2)}) async-start(), calls=%async_computation | async-start | bytes 7864320 | tf_op jit(solution)/shard_map/all_gather | solution.py:66
Sparse Core Ops, SparseCore 0:
  8.9 117.5 all-gather.2
where the time goes:
time: 155 us
  waiting for transfers between devices  120 us (77%)
  matrix products  20.1 us (13%)
  between operations  13.4 us (9%)
  local copies, waits for them, and re-layouts  1.57 us (1%)
    all_gather x1, waiting for transfers between devices, on_device_columns(): gathered = lax.all_gather(iterate[0], 'fsdp', axis=1, tiled=True)  119 us
    dot_general x1, matrix products, on_device_columns(): lax.dot_general(gathered, gathered, (((0,), (0,)), ((), ())), preferred_e...  12 us
    dot_general x1, matrix products, on_device_columns(): jnp.dot(gathered, mixing.astype(jnp.bfloat16), preferred_element_type=jnp...  8.06 us
  transfers between devices with their start and end apart: 1, of which 1 were waited for; matrix products, arithmetic and copies ran while one was open for 0% of the time, Pallas kernels for 0%

commit v1 on v0

--- a/solution.py
+++ b/solution.py
@@ -63,7 +63,25 @@
     own = lax.axis_index("fsdp")
     _, rows_all, columns = iterate.shape
     out_scale = 0.2 * math.sqrt(max(rows_all, columns * devices))
-    gathered = lax.all_gather(iterate[0], "fsdp", axis=1, tiled=True)
+    count, index, extent = (lax.axis_size("fsdp"), lax.axis_index("fsdp"), iterate[0].shape[1])
+    ahead = [(i, (i + 1) % count) for i in range(count)]
+    backward = [(i, (i - 1) % count) for i in range(count)]
+    gathered = jnp.zeros(
+        (*iterate[0].shape[:1], count * extent, *iterate[0].shape[1 + 1 :]), iterate[0].dtype
+    )
+    gathered = lax.dynamic_update_slice_in_dim(gathered, iterate[0], index * extent, axis=1)
+    from_left = from_right = iterate[0]
+    half = count // 2
+    for step in range(1, half + 1):
+        from_left = lax.ppermute(from_left, "fsdp", ahead)
+        gathered = lax.dynamic_update_slice_in_dim(
+            gathered, from_left, (index - step) % count * extent, axis=1
+        )
+        if step < count - half:
+            from_right = lax.ppermute(from_right, "fsdp", backward)
+            gathered = lax.dynamic_update_slice_in_dim(
+                gathered, from_right, (index + step) % count * extent, axis=1
+            )
     gram = lax.dot_general(
         gathered, gathered, (((0,), (0,)), ((), ())), preferred_element_type=jnp.float32
     )

time: 155 us -> 128 us (0.83)
  waiting for transfers between devices: 120 us -> 99.1 us
  between operations: 13.4 us -> 0.06 us
  starting transfers between devices: 0.01 us -> 5.1 us
  local copies, waits for them, and re-layouts: 1.57 us -> 5.81 us
  matrix products: 20.1 us -> 17.5 us
    all_gather x1 -> x0, waiting for transfers between devices: 119 us -> none  [on_device_columns(): gathered = lax.all_gather(iterate[0], 'fsdp', axis=1, tiled=True)]
    ppermute x0 -> x3, waiting for transfers between devices: none -> 99.1 us  [the longest x2 68 us: on_device_columns(): from_left = lax.ppermute(from_left, 'fsdp', ahead)]
    ppermute x0 -> x3, starting transfers between devices: none -> 5.1 us  [the longest x2 3.03 us: on_device_columns(): from_left = lax.ppermute(from_left, 'fsdp', ahead)]
    dot_general x1, matrix products: 12 us -> 8.32 us  [on_device_columns(): lax.dot_general(gathered, gathered, (((0,), (0,)), ((), ())), preferred_e...]
    unnamed x0 -> x4, local copies, waits for them, and re-layouts: none -> 2.65 us
    dynamic_update_slice x0 -> x4, local copies, waits for them, and re-layouts: none -> 2.37 us  [the longest x1 1.65 us: on_device_columns(): lax.dynamic_update_slice_in_dim(gathered, from_right, (index + step) % co...]
  transfers between devices with their start and end apart: 1 -> 3, of which waited for: 1 -> 3; matrix products, arithmetic and copies ran while one was open for 0% -> 2% of each run, Pallas kernels for 0% -> 0%
where the time goes in v1:
time: 128 us
  waiting for transfers between devices  99.1 us (77%)
  matrix products  17.5 us (14%)
  local copies, waits for them, and re-layouts  5.81 us (5%)
  starting transfers between devices  5.1 us (4%)
    ppermute x2, waiting for transfers between devices, on_device_columns(): from_left = lax.ppermute(from_left, 'fsdp', ahead)  68 us
    ppermute x1, waiting for transfers between devices, on_device_columns(): from_right = lax.ppermute(from_right, 'fsdp', backward)  31.1 us
    dot_general x1, matrix products, on_device_columns(): jnp.dot(gathered, mixing.astype(jnp.bfloat16), preferred_element_type=jnp...  9.2 us
    dot_general x1, matrix products, on_device_columns(): lax.dot_general(gathered, gathered, (((0,), (0,)), ((), ())), preferred_e...  8.32 us
    ppermute x2, starting transfers between devices, on_device_columns(): from_left = lax.ppermute(from_left, 'fsdp', ahead)  3.03 us
    unnamed x4, local copies, waits for them, and re-layouts  2.65 us
  transfers between devices with their start and end apart: 3, of which 3 were waited for; matrix products, arithmetic and copies ran while one was open for 2% of the time, Pallas kernels for 0%

profile of v1, /device:TPU:0, one launch (start us, length us, event | category | flops | bytes accessed | tf_op | source)
XLA Modules:
  0.0 127.6 jit_solution(971018339744226650)
XLA Ops:
  0.0 0.0 copy-start.1
  0.0 3.0 %collective-permute-start = (bf16[3072,256]{1,0:T(8,128)(2,1)}, bf16[3072,256]{1,0:T(8,128)(2,1)S(1)}, u32[]{:S(2)}, u32[]{:S(2)}) collective-permute-start(bf16[3072,256]{1,0:T(8,128)(2,1)} %bitcast.7), channel_id=1, source_target_pairs={{0,4},{4,8},{8,12},{12,0},{1,5},{5,9},{9,13},{13,1},{2,6},{6,10},{... | collective-permute-start | bytes 4718600 | tf_op jit(solution)/shard_map/ppermute | solution.py:76
  3.0 2.1 %collective-permute-start.1 = (bf16[3072,256]{1,0:T(8,128)(2,1)}, bf16[3072,256]{1,0:T(8,128)(2,1)}, u32[]{:S(2)}, u32[]{:S(2)}) collective-permute-start(bf16[3072,256]{1,0:T(8,128)(2,1)} %bitcast.8), channel_id=1, source_target_pairs={{0,12},{4,0},{8,4},{12,8},{1,13},{5,1},{9,5},{13,9},{2,14},{6,2},{... | collective-permute-start | bytes 4718600 | tf_op jit(solution)/shard_map/ppermute | solution.py:81
  5.1 35.5 %collective-permute-done = bf16[3072,256]{1,0:T(8,128)(2,1)S(1)} collective-permute-done((bf16[3072,256]{1,0:T(8,128)(2,1)}, bf16[3072,256]{1,0:T(8,128)(2,1)S(1)}, u32[]{:S(2)}, u32[]{:S(2)}) %collective-permute-start) | collective-permute-done | bytes 1572896 | tf_op jit(solution)/shard_map/ppermute | solution.py:76
  40.6 0.0 collective-permute-start.2
  40.6 0.8 broadcast_in_dim.6
  41.4 0.0 copy-done.1
  41.4 0.2 constant_dynamic-update-slice_fusion.3
  41.7 0.2 constant_dynamic-update-slice_fusion.2
  41.9 31.1 %collective-permute-done.1 = bf16[3072,256]{1,0:T(8,128)(2,1)} collective-permute-done((bf16[3072,256]{1,0:T(8,128)(2,1)}, bf16[3072,256]{1,0:T(8,128)(2,1)}, u32[]{:S(2)}, u32[]{:S(2)}) %collective-permute-start.1) | collective-permute-done | bytes 1572896 | tf_op jit(solution)/shard_map/ppermute | solution.py:81
  73.1 1.6 %constant_dynamic-update-slice_fusion.1 = bf16[3072,1024]{1,0:T(8,128)(2,1)S(1)} fusion(bf16[3072,1024]{1,0:T(8,128)(2,1)S(1)} %constant_dynamic-update-slice_fusion.2, bf16[3072,256]{1,0:T(8,128)(2,1)} %collective-permute-done.1, s32[]{:T(128)S(6)} %select_n.32), kind=kLoop, calls=%fused_computation.12 | loop fusion | bytes 3145732 | tf_op jit(solution)/shard_map/dynamic_update_slice | solution.py:82
  74.7 32.5 %collective-permute-done.2 = bf16[3072,256]{1,0:T(8,128)(2,1)S(1)} collective-permute-done((bf16[3072,256]{1,0:T(8,128)(2,1)S(1)}, bf16[3072,256]{1,0:T(8,128)(2,1)S(1)}, u32[]{:S(2)}, u32[]{:S(2)}) %collective-permute-start.2) | collective-permute-done | bytes 1572896 | tf_op jit(solution)/shard_map/ppermute | solution.py:76
  107.2 0.2 constant_dynamic-update-slice_fusion
  107.4 0.0 copy-start
  107.4 2.6 %copy-done = bf16[3072,1024]{1,0:T(8,128)(2,1)} copy-done((bf16[3072,1024]{1,0:T(8,128)(2,1)}, bf16[3072,1024]{1,0:T(8,128)(2,1)S(1)}, u32[]{:S(2)}) %copy-start) | copy-done | bytes 6291480
  110.1 8.3 %fusion.19 = f32[1024,1024]{1,0:T(8,128)} fusion(bf16[3072,1024]{1,0:T(8,128)(2,1)S(1)} %constant_dynamic-update-slice_fusion), kind=kOutput, calls=%fused_computation.21 | convolution fusion | flops 6442450944 | bytes 10485760 | tf_op jit(solution)/shard_map/dot_general | solution.py:85
  118.4 9.2 %fusion = bf16[1,3072,256]{2,1,0:T(8,128)(2,1)} fusion(bf16[3072,1024]{1,0:T(8,128)(2,1)} %copy-done, f32[1024,1024]{1,0:T(8,128)} %fusion.19, s32[]{:T(128)S(6)} %select_n.28, s32[256]{0:T(256)S(1)} %iota_add_fusion), kind=kOutput, calls=%fused_computation.1 | convolution fusion | flops 2151677952 | bytes 14157824 | tf_op jit(solution)/shard_map/dot_general | solution.py:95
  (1 shorter events, 0.0 us)
Async XLA Ops:
  0.0 41.4 %copy-start.1 = (bf16[1,3072,256]{2,1,0:T(8,128)(2,1)S(1)}, bf16[1,3072,256]{2,1,0:T(8,128)(2,1)}, u32[]{:S(2)}) copy-start(bf16[1,3072,256]{2,1,0:T(8,128)(2,1)} %param.1) | copy-start | bytes 4718596
  0.0 40.6 %collective-permute-start = (bf16[3072,256]{1,0:T(8,128)(2,1)}, bf16[3072,256]{1,0:T(8,128)(2,1)S(1)}, u32[]{:S(2)}, u32[]{:S(2)}) collective-permute-start(bf16[3072,256]{1,0:T(8,128)(2,1)} %bitcast.7), channel_id=1, source_target_pairs={{0,4},{4,8},{8,12},{12,0},{1,5},{5,9},{9,13},{13,1},{2,6},{6,10},{... | collective-permute-start | bytes 4718600 | tf_op jit(solution)/shard_map/ppermute | solution.py:76
  3.0 70.0 %collective-permute-start.1 = (bf16[3072,256]{1,0:T(8,128)(2,1)}, bf16[3072,256]{1,0:T(8,128)(2,1)}, u32[]{:S(2)}, u32[]{:S(2)}) collective-permute-start(bf16[3072,256]{1,0:T(8,128)(2,1)} %bitcast.8), channel_id=1, source_target_pairs={{0,12},{4,0},{8,4},{12,8},{1,13},{5,1},{9,5},{13,9},{2,14},{6,2},{... | collective-permute-start | bytes 4718600 | tf_op jit(solution)/shard_map/ppermute | solution.py:81
  40.6 66.6 %collective-permute-start.2 = (bf16[3072,256]{1,0:T(8,128)(2,1)S(1)}, bf16[3072,256]{1,0:T(8,128)(2,1)S(1)}, u32[]{:S(2)}, u32[]{:S(2)}) collective-permute-start(bf16[3072,256]{1,0:T(8,128)(2,1)S(1)} %collective-permute-done), channel_id=1, source_target_pairs={{0,4},{4,8},{8,12},{12,0},{1,5},{5,9},{9,13},{13,1},{2,6},{6,10},{... | collective-permute-start | bytes 4718600 | tf_op jit(solution)/shard_map/ppermute | solution.py:76
  107.4 2.7 %copy-start = (bf16[3072,1024]{1,0:T(8,128)(2,1)}, bf16[3072,1024]{1,0:T(8,128)(2,1)S(1)}, u32[]{:S(2)}) copy-start(bf16[3072,1024]{1,0:T(8,128)(2,1)S(1)} %constant_dynamic-update-slice_fusion) | copy-start | bytes 18874372
